TPU v7x, 32 devices: a whole 2x2x4 slice. The times are simulated.
32 devices in a mesh: slab: 8 (over z, x), row: 4 (over y, core).
Axes of the slice: x: 2, y: 2, z: 4, core: 2. Of those that a mesh axis runs over, the one named last changes fastest.
Arguments:
- edge_weights: int32 [3, 16, 32, 512], P(None, 'slab', 'row'), may hold values from 1 to 15
- seeds: int32 [16, 32, 512], P('slab', 'row'), may hold values from -8 to 7
- supervoxel: int32 [16, 32, 512], P('slab', 'row'), may hold values from 0 to 127
- coarse_blocks: float32 [4, 1024, 1024], P('row', 'slab'), as said below
Outputs:
- potentials: float32 [8, 16, 32, 512], P(None, 'slab', 'row')
Inputs may be any that keep to these rules, and one draw needn't show every extreme that they name: `seeds`: a negative value marks an unseeded voxel. `coarse_blocks`: the entries named by dc lie between 0.6 and 1.2 times 2 * 8 * 4.
All inputs are finite; a program needn't handle non-finite values.
Results may differ from a plain program's by a relative error of at most 0.00024.
Values sent between devices are 32-bit elements; how exact they have to be, the bound alone decides.
No kernel may reach another device: no remote copies, remote signals or barrier semaphores. Data moves between devices by JAX's collectives and lax.ppermute only.
A program may use at most 64 MiB of HBM per device.

v0:
```python
import math
import jax
import jax.numpy as jnp
from jax import lax
from jax.sharding import PartitionSpec as P

LABELS = 8
CZ = 2
CY = 8
NX = 512
CC = 128
CYCLES = 2
prior_mass = 0.25
seed_weight = 4.0
smooth_step = 0.8
coarse_step = 0.7
weight_unit = 0.125


def padded(cells, sides, width):
    for axis, dim in sides:
        count = lax.axis_size(axis)
        ends = count - 1
        head = lax.slice_in_dim(cells, 0, width, axis=dim)
        tail = lax.slice_in_dim(cells, cells.shape[dim] - width, cells.shape[dim], axis=dim)
        cells = jnp.concatenate(
            [
                lax.ppermute(tail, axis, [(i, (i + 1) % count) for i in range(ends)]),
                cells,
                lax.ppermute(head, axis, [((i + 1) % count, i) for i in range(ends)]),
            ],
            axis=dim,
        )
    return cells


def shifted(block, axis, distance):
    devices = range(lax.axis_size(axis))
    route = [(i - distance, i) for i in devices if i - distance in devices]
    return lax.ppermute(block, axis, route)


def lower_x(a):
    return jnp.pad(a[..., :-1], [(0, 0)] * (a.ndim - 1) + [(1, 0)])


def upper_x(a):
    return jnp.pad(a[..., 1:], [(0, 0)] * (a.ndim - 1) + [(0, 1)])


def crop(a, margin):
    return a[..., margin : a.shape[-3] - margin, margin : a.shape[-2] - margin, :]


def rim_one(field):
    return padded(field, (("slab", 1), ("row", 2)), 1)


def per_device(edge_weights, seeds, supervoxel, coarse_blocks):
    n_slab = lax.axis_size("slab")
    n_row = lax.axis_size("row")
    group = min(16, n_slab)
    sections = n_slab // group
    slab_pos = lax.axis_index("slab")
    row_pos = lax.axis_index("row")
    stacked = jnp.concatenate([edge_weights, seeds[None]], axis=0)
    lower_plane = shifted(edge_weights[0, -1:], "slab", 1)
    lower_row = shifted(edge_weights[1, :, -1:], "row", 1)
    framed = jnp.pad(stacked, ((0, 0), (1, 1), (1, 1), (0, 0)))
    framed = framed.at[0, :1, 1:-1].set(lower_plane)
    framed = framed.at[1, 1:-1, :1].set(lower_row)
    width = (framed.shape[1] - CZ) // 2
    weights = framed[:3].astype(jnp.float32) * weight_unit
    plane_ids = slab_pos * CZ - width + jnp.arange(CZ + 2 * width, dtype=jnp.int32)
    line_ids = row_pos * CY - width + jnp.arange(CY + 2 * width, dtype=jnp.int32)
    keep_z = (plane_ids != CZ * n_slab - 1).astype(jnp.float32)[:, None, None]
    keep_y = (line_ids != CY * n_row - 1).astype(jnp.float32)[None, :, None]
    keep_x = (jnp.arange(NX) < NX - 1).astype(jnp.float32)[None, None, :]
    w_z = weights[0] * keep_z
    w_y = weights[1] * keep_y
    w_x = weights[2] * keep_x
    seed_inner = crop(framed[3], 1)
    inner_x = crop(w_x, 1)
    diag = (
        prior_mass
        + seed_weight * (seed_inner >= 0).astype(jnp.float32)
        + crop(w_z, 1)
        + crop(w_y, 1)
        + inner_x
        + w_z[:-2, 1:-1]
        + w_y[1:-1, :-2]
        + lower_x(inner_x)
    )
    label_ids = jnp.arange(LABELS, dtype=jnp.int32)
    source = seed_weight * (seed_inner[None] == label_ids[:, None, None, None]).astype(jnp.float32)

    def residual_on(frame, rim):
        margin = width - rim - 1
        face_z = crop(w_z, margin)
        face_y = crop(w_y, margin)
        face_x = crop(w_x, margin)[1:-1, 1:-1]
        centre = frame[:, 1:-1, 1:-1]
        near = face_z[1:-1, 1:-1] * frame[:, 2:, 1:-1] + face_z[:-2, 1:-1] * frame[:, :-2, 1:-1]
        near = (
            near + face_y[1:-1, 1:-1] * frame[:, 1:-1, 2:] + face_y[1:-1, :-2] * frame[:, 1:-1, :-2]
        )
        near = near + face_x * upper_x(centre) + lower_x(face_x) * lower_x(centre)
        local_diag = crop(diag, width - 1 - rim)
        local_source = crop(source, width - 1 - rim)
        return (local_source - (local_diag * centre - near), local_diag, centre)

    def sweep(field):
        change, local_diag, centre = residual_on(rim_one(field), 0)
        return centre + smooth_step * change / local_diag

    block_row = coarse_blocks[0]
    turn = slab_pos // sections
    section_id = slab_pos % sections
    own_block = lax.dynamic_slice_in_dim(block_row, turn * CC, CC, 1)
    coarse_diag = jnp.diagonal(own_block)
    cells = CZ * CY * NX
    span = math.gcd(cells, 2048)
    flat_ids = supervoxel.reshape(cells)
    coarse_ids = jnp.arange(CC, dtype=jnp.int32)
    field = jnp.zeros((LABELS, CZ, CY, NX), jnp.float32)
    for cycle in range(CYCLES):
        field = sweep(sweep(field))
        residual, unused_diag, unused_centre = residual_on(rim_one(field), 0)
        flat_rows = residual.reshape(LABELS, cells)

        def collect_block(index, total):
            piece = lax.dynamic_slice_in_dim(flat_rows, index * span, span, 1)
            piece_ids = lax.dynamic_slice_in_dim(flat_ids, index * span, span, 0)
            onehot = (piece_ids[:, None] == coarse_ids[None, :]).astype(jnp.float32)
            return total + jnp.dot(
                piece, onehot, precision=lax.Precision.HIGHEST, preferred_element_type=jnp.float32
            )

        coarse_rhs = lax.fori_loop(
            0, cells // span, collect_block, jnp.zeros((LABELS, CC), jnp.float32)
        )
        first = coarse_step * coarse_rhs / coarse_diag
        gathered = lax.all_gather(first, "slab", axis=1, tiled=True)
        arranged = gathered.reshape(LABELS, group, sections, CC)
        section = lax.dynamic_slice_in_dim(arranged, section_id, 1, 2).reshape(LABELS, group * CC)
        second = (
            first
            + coarse_step
            * (
                coarse_rhs
                - lax.dot_general(
                    section,
                    block_row,
                    (((1,), (1,)), ((), ())),
                    precision=lax.Precision.HIGHEST,
                    preferred_element_type=jnp.float32,
                )
            )
            / coarse_diag
        )
        correction = jnp.take(second, flat_ids, axis=1).reshape(LABELS, CZ, CY, NX)
        field = sweep(field + correction)
    return field


def solution(mesh):
    in_specs = (
        P(None, "slab", "row", None),
        P("slab", "row", None),
        P("slab", "row", None),
        P("row", "slab", None),
    )
    out_specs = P(None, "slab", "row", None)
    return jax.shard_map(
        per_device, mesh=mesh, in_specs=in_specs, out_specs=out_specs, check_vma=False
    )
```

profile of v0, /device:TPU:6, one launch (start us, length us, event | category | flops | bytes accessed | tf_op | source)
XLA Modules:
  0.0 296.9 jit_solution(196694166765577341)
XLA Ops:
  2.6 4.3 %collective-permute-start.3 = (f32[8,1,8,512]{3,2,1,0:T(8,128)S(1)}, f32[8,1,8,512]{3,2,1,0:T(8,128)S(1)}, u32[]{:S(2)}, u32[]{:S(2)}) collective-permute-start(f32[8,1,8,512]{3,2,1,0:T(8,128)S(1)} %broadcast.145), channel_id=1, source_target_pairs={{0,4},{4,8},{8,12},{12,16},{16,20},{20,24},{24,28},{1,5},{5,9},{9,... | collective-permute-start | bytes 393224 | tf_op jit(solution)/shard_map/ppermute | solution.py:28
  16.7 3.6 %collective-permute-start.4 = (f32[8,4,1,512]{3,2,1,0:T(1,128)S(1)}, f32[8,4,1,512]{3,2,1,0:T(1,128)S(1)}, u32[]{:S(2)}, u32[]{:S(2)}) collective-permute-start(f32[8,4,1,512]{3,2,1,0:T(1,128)S(1)} %get-tuple-element.286), channel_id=1, source_target_pairs={{1,0},{2,1},{3,2},{5,4},{6,5},{7,6},{9,8},{10,9},{11,10},{13,12},{... | collective-permute-start | bytes 196616 | tf_op jit(solution)/shard_map/ppermute | solution.py:30
  22.4 3.6 %collective-permute-done.5 = f32[8,4,1,512]{3,2,1,0:T(1,128)S(1)} collective-permute-done((f32[8,4,1,512]{3,2,1,0:T(1,128)S(1)}, f32[8,4,1,512]{3,2,1,0:T(1,128)S(1)}, u32[]{:S(2)}, u32[]{:S(2)}) %collective-permute-start.5) | collective-permute-done | bytes 65568 | tf_op jit(solution)/shard_map/ppermute | solution.py:28
  26.2 3.3 %collective-permute-start.6 = (f32[8,1,8,512]{3,2,1,0:T(8,128)S(1)}, f32[8,1,8,512]{3,2,1,0:T(8,128)S(1)}, u32[]{:S(2)}, u32[]{:S(2)}) collective-permute-start(f32[8,1,8,512]{3,2,1,0:T(8,128)S(1)} %get-tuple-element.318), channel_id=1, source_target_pairs={{4,0},{8,4},{12,8},{16,12},{20,16},{24,20},{28,24},{5,1},{9,5},{13... | collective-permute-start | bytes 393224 | tf_op jit(solution)/shard_map/ppermute | solution.py:30
  29.5 3.5 %collective-permute-start.7 = (f32[8,1,8,512]{3,2,1,0:T(8,128)S(1)}, f32[8,1,8,512]{3,2,1,0:T(8,128)S(1)}, u32[]{:S(2)}, u32[]{:S(2)}) collective-permute-start(f32[8,1,8,512]{3,2,1,0:T(8,128)S(1)} %get-tuple-element.317), channel_id=1, source_target_pairs={{0,4},{4,8},{8,12},{12,16},{16,20},{20,24},{24,28},{1,5},{5,9},{9,... | collective-permute-start | bytes 393224 | tf_op jit(solution)/shard_map/ppermute | solution.py:28
  41.0 3.0 %collective-permute-done.9 = f32[8,4,1,512]{3,2,1,0:T(1,128)S(1)} collective-permute-done((f32[8,4,1,512]{3,2,1,0:T(1,128)S(1)}, f32[8,4,1,512]{3,2,1,0:T(1,128)S(1)}, u32[]{:S(2)}, u32[]{:S(2)}) %collective-permute-start.9) | collective-permute-done | bytes 65568 | tf_op jit(solution)/shard_map/ppermute | solution.py:28
  46.2 4.8 %collective-permute-start.11 = (f32[8,1,8,512]{3,2,1,0:T(8,128)S(1)}, f32[8,1,8,512]{3,2,1,0:T(8,128)S(1)}, u32[]{:S(2)}, u32[]{:S(2)}) collective-permute-start(f32[8,1,8,512]{3,2,1,0:T(8,128)S(1)} %get-tuple-element.313), channel_id=1, source_target_pairs={{0,4},{4,8},{8,12},{12,16},{16,20},{20,24},{24,28},{1,5},{5,9},{9,... | collective-permute-start | bytes 393224 | tf_op jit(solution)/shard_map/ppermute | solution.py:28
  58.1 3.0 %collective-permute-done.13 = f32[8,4,1,512]{3,2,1,0:T(1,128)S(1)} collective-permute-done((f32[8,4,1,512]{3,2,1,0:T(1,128)S(1)}, f32[8,4,1,512]{3,2,1,0:T(1,128)S(1)}, u32[]{:S(2)}, u32[]{:S(2)}) %collective-permute-start.13) | collective-permute-done | bytes 65568 | tf_op jit(solution)/shard_map/ppermute | solution.py:28
  64.1 31.9 %all_gather.6 = f32[8,1024]{1,0:T(8,128)S(1)} all-gather(f32[8,128]{1,0:T(8,128)S(1)} %multiply_divide_fusion.1), channel_id=1, replica_groups=mesh['slab'=8,'row'=4] {'slab'}, dimensions={1}, use_global_device_ids=true | all-gather | bytes 36864 | tf_op jit(solution)/shard_map/all_gather | solution.py:143
  96.6 27.9 %gather_fusion.1 = f32[8192,8]{1,0:T(8,128)} fusion(f32[8,128]{0,1:T(8,128)S(1)} %copy.9, s32[8192]{0:T(1024)S(1)} %fusion.122), kind=kCustom, calls=%fused_computation.clone | custom fusion | bytes 557056 | tf_op jit(solution)/shard_map/jit(_take)/gather | solution.py:161
  124.5 7.5 %broadcast_select_fusion.1 = f32[8192,8]{1,0:T(8,128)} fusion(f32[8192,8]{1,0:T(8,128)} %gather_fusion.1, pred[8192]{0:T(1024)(128)(4,1)S(1)} %compare_and_fusion), kind=kLoop, calls=%fused_computation.16 | loop fusion | flops 65536 | bytes 532480 | tf_op jit(solution)/shard_map/jit(_take)/select_n | solution.py:161
  134.8 3.3 %collective-permute-start.14 = (f32[8,1,8,512]{3,2,1,0:T(8,128)S(1)}, f32[8,1,8,512]{3,2,1,0:T(8,128)S(1)}, u32[]{:S(2)}, u32[]{:S(2)}) collective-permute-start(f32[8,1,8,512]{3,2,1,0:T(8,128)S(1)} %get-tuple-element.310), channel_id=1, source_target_pairs={{4,0},{8,4},{12,8},{16,12},{20,16},{24,20},{28,24},{5,1},{9,5},{13... | collective-permute-start | bytes 393224 | tf_op jit(solution)/shard_map/ppermute | solution.py:30
  138.1 3.5 %collective-permute-start.15 = (f32[8,1,8,512]{3,2,1,0:T(8,128)S(1)}, f32[8,1,8,512]{3,2,1,0:T(8,128)S(1)}, u32[]{:S(2)}, u32[]{:S(2)}) collective-permute-start(f32[8,1,8,512]{3,2,1,0:T(8,128)S(1)} %get-tuple-element.309), channel_id=1, source_target_pairs={{0,4},{4,8},{8,12},{12,16},{16,20},{20,24},{24,28},{1,5},{5,9},{9,... | collective-permute-start | bytes 393224 | tf_op jit(solution)/shard_map/ppermute | solution.py:28
  149.6 3.0 %collective-permute-done.17 = f32[8,4,1,512]{3,2,1,0:T(1,128)S(1)} collective-permute-done((f32[8,4,1,512]{3,2,1,0:T(1,128)S(1)}, f32[8,4,1,512]{3,2,1,0:T(1,128)S(1)}, u32[]{:S(2)}, u32[]{:S(2)}) %collective-permute-start.17) | collective-permute-done | bytes 65568 | tf_op jit(solution)/shard_map/ppermute | solution.py:28
  154.8 4.8 %collective-permute-start.19 = (f32[8,1,8,512]{3,2,1,0:T(8,128)S(1)}, f32[8,1,8,512]{3,2,1,0:T(8,128)S(1)}, u32[]{:S(2)}, u32[]{:S(2)}) collective-permute-start(f32[8,1,8,512]{3,2,1,0:T(8,128)S(1)} %get-tuple-element.305), channel_id=1, source_target_pairs={{0,4},{4,8},{8,12},{12,16},{16,20},{20,24},{24,28},{1,5},{5,9},{9,... | collective-permute-start | bytes 393224 | tf_op jit(solution)/shard_map/ppermute | solution.py:28
  166.7 3.0 %collective-permute-done.21 = f32[8,4,1,512]{3,2,1,0:T(1,128)S(1)} collective-permute-done((f32[8,4,1,512]{3,2,1,0:T(1,128)S(1)}, f32[8,4,1,512]{3,2,1,0:T(1,128)S(1)}, u32[]{:S(2)}, u32[]{:S(2)}) %collective-permute-start.21) | collective-permute-done | bytes 65568 | tf_op jit(solution)/shard_map/ppermute | solution.py:28
  172.0 5.3 %collective-permute-start.23 = (f32[8,1,8,512]{3,2,1,0:T(8,128)S(1)}, f32[8,1,8,512]{3,2,1,0:T(8,128)S(1)}, u32[]{:S(2)}, u32[]{:S(2)}) collective-permute-start(f32[8,1,8,512]{3,2,1,0:T(8,128)S(1)} %get-tuple-element.301), channel_id=1, source_target_pairs={{0,4},{4,8},{8,12},{12,16},{16,20},{20,24},{24,28},{1,5},{5,9},{9,... | collective-permute-start | bytes 393224 | tf_op jit(solution)/shard_map/ppermute | solution.py:28
  189.7 5.2 %collective-permute-start.27 = (f32[8,1,8,512]{3,2,1,0:T(8,128)S(1)}, f32[8,1,8,512]{3,2,1,0:T(8,128)S(1)}, u32[]{:S(2)}, u32[]{:S(2)}) collective-permute-start(f32[8,1,8,512]{3,2,1,0:T(8,128)S(1)} %get-tuple-element.297), channel_id=1, source_target_pairs={{0,4},{4,8},{8,12},{12,16},{16,20},{20,24},{24,28},{1,5},{5,9},{9,... | collective-permute-start | bytes 393224 | tf_op jit(solution)/shard_map/ppermute | solution.py:28
  208.0 30.0 %all_gather.7 = f32[8,1024]{1,0:T(8,128)S(1)} all-gather(f32[8,128]{1,0:T(8,128)S(1)} %multiply_divide_fusion), channel_id=1, replica_groups=mesh['slab'=8,'row'=4] {'slab'}, dimensions={1}, use_global_device_ids=true | all-gather | bytes 36864 | tf_op jit(solution)/shard_map/all_gather | solution.py:143
  238.6 27.9 %gather_fusion.2 = f32[8192,8]{1,0:T(8,128)} fusion(f32[8,128]{0,1:T(8,128)S(1)} %copy.11, s32[8192]{0:T(1024)S(1)} %fusion.122), kind=kCustom, calls=%fused_computation.1.clone | custom fusion | bytes 557056 | tf_op jit(solution)/shard_map/jit(_take)/gather | solution.py:161
  266.5 7.5 %broadcast_select_fusion = f32[8192,8]{1,0:T(8,128)} fusion(f32[8192,8]{1,0:T(8,128)} %gather_fusion.2, pred[8192]{0:T(1024)(128)(4,1)S(1)} %compare_and_fusion), kind=kLoop, calls=%fused_computation.15 | loop fusion | flops 65536 | bytes 532480 | tf_op jit(solution)/shard_map/jit(_take)/select_n | solution.py:161
  276.8 4.6 %collective-permute-start.30 = (f32[8,1,8,512]{3,2,1,0:T(8,128)S(1)}, f32[8,1,8,512]{3,2,1,0:T(8,128)S(1)}, u32[]{:S(2)}, u32[]{:S(2)}) collective-permute-start(f32[8,1,8,512]{3,2,1,0:T(8,128)S(1)} %get-tuple-element.294), channel_id=1, source_target_pairs={{4,0},{8,4},{12,8},{16,12},{20,16},{24,20},{28,24},{5,1},{9,5},{13... | collective-permute-start | bytes 393224 | tf_op jit(solution)/shard_map/ppermute | solution.py:30
  284.6 3.7 %collective-permute-done.31 = f32[8,1,8,512]{3,2,1,0:T(8,128)S(1)} collective-permute-done((f32[8,1,8,512]{3,2,1,0:T(8,128)S(1)}, f32[8,1,8,512]{3,2,1,0:T(8,128)S(1)}, u32[]{:S(2)}, u32[]{:S(2)}) %collective-permute-start.31) | collective-permute-done | bytes 131104 | tf_op jit(solution)/shard_map/ppermute | solution.py:28
  292.9 3.0 %collective-permute-done.33 = f32[8,4,1,512]{3,2,1,0:T(1,128)S(1)} collective-permute-done((f32[8,4,1,512]{3,2,1,0:T(1,128)S(1)}, f32[8,4,1,512]{3,2,1,0:T(1,128)S(1)}, u32[]{:S(2)}, u32[]{:S(2)}) %collective-permute-start.33) | collective-permute-done | bytes 65568 | tf_op jit(solution)/shard_map/ppermute | solution.py:28
  (139 shorter events, 99.8 us)
Async XLA Ops:
  0.0 16.5 %collective-permute-start.2 = (f32[8,1,8,512]{3,2,1,0:T(8,128)S(1)}, f32[8,1,8,512]{3,2,1,0:T(8,128)S(1)}, u32[]{:S(2)}, u32[]{:S(2)}) collective-permute-start(f32[8,1,8,512]{3,2,1,0:T(8,128)S(1)} %broadcast.145), channel_id=1, source_target_pairs={{4,0},{8,4},{12,8},{16,12},{20,16},{24,20},{28,24},{5,1},{9,5},{13... | collective-permute-start | bytes 393224 | tf_op jit(solution)/shard_map/ppermute | solution.py:30
  2.6 14.0 %collective-permute-start.3 = (f32[8,1,8,512]{3,2,1,0:T(8,128)S(1)}, f32[8,1,8,512]{3,2,1,0:T(8,128)S(1)}, u32[]{:S(2)}, u32[]{:S(2)}) collective-permute-start(f32[8,1,8,512]{3,2,1,0:T(8,128)S(1)} %broadcast.145), channel_id=1, source_target_pairs={{0,4},{4,8},{8,12},{12,16},{16,20},{20,24},{24,28},{1,5},{5,9},{9,... | collective-permute-start | bytes 393224 | tf_op jit(solution)/shard_map/ppermute | solution.py:28
  7.6 8.4 %collective-permute-start = (s32[1,8,512]{2,1,0:T(8,128)S(1)}, s32[1,8,512]{2,1,0:T(8,128)S(1)}, u32[]{:S(2)}, u32[]{:S(2)}) collective-permute-start(s32[1,8,512]{2,1,0:T(8,128)S(1)} %slice_bitcast_fusion.4), channel_id=1, source_target_pairs={{0,4},{4,8},{8,12},{12,16},{16,20},{20,24},{24,28},{1,5},{5,9},{9,... | collective-permute-start | bytes 49160 | tf_op jit(solution)/shard_map/ppermute | solution.py:40
  16.7 5.7 %collective-permute-start.4 = (f32[8,4,1,512]{3,2,1,0:T(1,128)S(1)}, f32[8,4,1,512]{3,2,1,0:T(1,128)S(1)}, u32[]{:S(2)}, u32[]{:S(2)}) collective-permute-start(f32[8,4,1,512]{3,2,1,0:T(1,128)S(1)} %get-tuple-element.286), channel_id=1, source_target_pairs={{1,0},{2,1},{3,2},{5,4},{6,5},{7,6},{9,8},{10,9},{11,10},{13,12},{... | collective-permute-start | bytes 196616 | tf_op jit(solution)/shard_map/ppermute | solution.py:30
  20.3 5.6 %collective-permute-start.5 = (f32[8,4,1,512]{3,2,1,0:T(1,128)S(1)}, f32[8,4,1,512]{3,2,1,0:T(1,128)S(1)}, u32[]{:S(2)}, u32[]{:S(2)}) collective-permute-start(f32[8,4,1,512]{3,2,1,0:T(1,128)S(1)} %get-tuple-element.287), channel_id=1, source_target_pairs={{0,1},{1,2},{2,3},{4,5},{5,6},{6,7},{8,9},{9,10},{10,11},{12,13},{... | collective-permute-start | bytes 196616 | tf_op jit(solution)/shard_map/ppermute | solution.py:28
  26.2 7.9 %collective-permute-start.6 = (f32[8,1,8,512]{3,2,1,0:T(8,128)S(1)}, f32[8,1,8,512]{3,2,1,0:T(8,128)S(1)}, u32[]{:S(2)}, u32[]{:S(2)}) collective-permute-start(f32[8,1,8,512]{3,2,1,0:T(8,128)S(1)} %get-tuple-element.318), channel_id=1, source_target_pairs={{4,0},{8,4},{12,8},{16,12},{20,16},{24,20},{28,24},{5,1},{9,5},{13... | collective-permute-start | bytes 393224 | tf_op jit(solution)/shard_map/ppermute | solution.py:30
  29.5 6.9 %collective-permute-start.7 = (f32[8,1,8,512]{3,2,1,0:T(8,128)S(1)}, f32[8,1,8,512]{3,2,1,0:T(8,128)S(1)}, u32[]{:S(2)}, u32[]{:S(2)}) collective-permute-start(f32[8,1,8,512]{3,2,1,0:T(8,128)S(1)} %get-tuple-element.317), channel_id=1, source_target_pairs={{0,4},{4,8},{8,12},{12,16},{16,20},{20,24},{24,28},{1,5},{5,9},{9,... | collective-permute-start | bytes 393224 | tf_op jit(solution)/shard_map/ppermute | solution.py:28
  38.4 5.6 %collective-permute-start.9 = (f32[8,4,1,512]{3,2,1,0:T(1,128)S(1)}, f32[8,4,1,512]{3,2,1,0:T(1,128)S(1)}, u32[]{:S(2)}, u32[]{:S(2)}) collective-permute-start(f32[8,4,1,512]{3,2,1,0:T(1,128)S(1)} %get-tuple-element.285), channel_id=1, source_target_pairs={{0,1},{1,2},{2,3},{4,5},{5,6},{6,7},{8,9},{9,10},{10,11},{12,13},{... | collective-permute-start | bytes 196616 | tf_op jit(solution)/shard_map/ppermute | solution.py:28
  44.3 7.8 %collective-permute-start.10 = (f32[8,1,8,512]{3,2,1,0:T(8,128)S(1)}, f32[8,1,8,512]{3,2,1,0:T(8,128)S(1)}, u32[]{:S(2)}, u32[]{:S(2)}) collective-permute-start(f32[8,1,8,512]{3,2,1,0:T(8,128)S(1)} %get-tuple-element.314), channel_id=1, source_target_pairs={{4,0},{8,4},{12,8},{16,12},{20,16},{24,20},{28,24},{5,1},{9,5},{13... | collective-permute-start | bytes 393224 | tf_op jit(solution)/shard_map/ppermute | solution.py:30
  46.2 7.3 %collective-permute-start.11 = (f32[8,1,8,512]{3,2,1,0:T(8,128)S(1)}, f32[8,1,8,512]{3,2,1,0:T(8,128)S(1)}, u32[]{:S(2)}, u32[]{:S(2)}) collective-permute-start(f32[8,1,8,512]{3,2,1,0:T(8,128)S(1)} %get-tuple-element.313), channel_id=1, source_target_pairs={{0,4},{4,8},{8,12},{12,16},{16,20},{20,24},{24,28},{1,5},{5,9},{9,... | collective-permute-start | bytes 393224 | tf_op jit(solution)/shard_map/ppermute | solution.py:28
  55.6 5.6 %collective-permute-start.13 = (f32[8,4,1,512]{3,2,1,0:T(1,128)S(1)}, f32[8,4,1,512]{3,2,1,0:T(1,128)S(1)}, u32[]{:S(2)}, u32[]{:S(2)}) collective-permute-start(f32[8,4,1,512]{3,2,1,0:T(1,128)S(1)} %get-tuple-element.283), channel_id=1, source_target_pairs={{0,1},{1,2},{2,3},{4,5},{5,6},{6,7},{8,9},{9,10},{10,11},{12,13},{... | collective-permute-start | bytes 196616 | tf_op jit(solution)/shard_map/ppermute | solution.py:28
  134.8 7.8 %collective-permute-start.14 = (f32[8,1,8,512]{3,2,1,0:T(8,128)S(1)}, f32[8,1,8,512]{3,2,1,0:T(8,128)S(1)}, u32[]{:S(2)}, u32[]{:S(2)}) collective-permute-start(f32[8,1,8,512]{3,2,1,0:T(8,128)S(1)} %get-tuple-element.310), channel_id=1, source_target_pairs={{4,0},{8,4},{12,8},{16,12},{20,16},{24,20},{28,24},{5,1},{9,5},{13... | collective-permute-start | bytes 393224 | tf_op jit(solution)/shard_map/ppermute | solution.py:30
  138.1 6.9 %collective-permute-start.15 = (f32[8,1,8,512]{3,2,1,0:T(8,128)S(1)}, f32[8,1,8,512]{3,2,1,0:T(8,128)S(1)}, u32[]{:S(2)}, u32[]{:S(2)}) collective-permute-start(f32[8,1,8,512]{3,2,1,0:T(8,128)S(1)} %get-tuple-element.309), channel_id=1, source_target_pairs={{0,4},{4,8},{8,12},{12,16},{16,20},{20,24},{24,28},{1,5},{5,9},{9,... | collective-permute-start | bytes 393224 | tf_op jit(solution)/shard_map/ppermute | solution.py:28
  147.0 5.6 %collective-permute-start.17 = (f32[8,4,1,512]{3,2,1,0:T(1,128)S(1)}, f32[8,4,1,512]{3,2,1,0:T(1,128)S(1)}, u32[]{:S(2)}, u32[]{:S(2)}) collective-permute-start(f32[8,4,1,512]{3,2,1,0:T(1,128)S(1)} %get-tuple-element.281), channel_id=1, source_target_pairs={{0,1},{1,2},{2,3},{4,5},{5,6},{6,7},{8,9},{9,10},{10,11},{12,13},{... | collective-permute-start | bytes 196616 | tf_op jit(solution)/shard_map/ppermute | solution.py:28
  152.9 7.8 %collective-permute-start.18 = (f32[8,1,8,512]{3,2,1,0:T(8,128)S(1)}, f32[8,1,8,512]{3,2,1,0:T(8,128)S(1)}, u32[]{:S(2)}, u32[]{:S(2)}) collective-permute-start(f32[8,1,8,512]{3,2,1,0:T(8,128)S(1)} %get-tuple-element.306), channel_id=1, source_target_pairs={{4,0},{8,4},{12,8},{16,12},{20,16},{24,20},{28,24},{5,1},{9,5},{13... | collective-permute-start | bytes 393224 | tf_op jit(solution)/shard_map/ppermute | solution.py:30
  154.8 7.3 %collective-permute-start.19 = (f32[8,1,8,512]{3,2,1,0:T(8,128)S(1)}, f32[8,1,8,512]{3,2,1,0:T(8,128)S(1)}, u32[]{:S(2)}, u32[]{:S(2)}) collective-permute-start(f32[8,1,8,512]{3,2,1,0:T(8,128)S(1)} %get-tuple-element.305), channel_id=1, source_target_pairs={{0,4},{4,8},{8,12},{12,16},{16,20},{20,24},{24,28},{1,5},{5,9},{9,... | collective-permute-start | bytes 393224 | tf_op jit(solution)/shard_map/ppermute | solution.py:28
  170.1 8.3 %collective-permute-start.22 = (f32[8,1,8,512]{3,2,1,0:T(8,128)S(1)}, f32[8,1,8,512]{3,2,1,0:T(8,128)S(1)}, u32[]{:S(2)}, u32[]{:S(2)}) collective-permute-start(f32[8,1,8,512]{3,2,1,0:T(8,128)S(1)} %get-tuple-element.302), channel_id=1, source_target_pairs={{4,0},{8,4},{12,8},{16,12},{20,16},{24,20},{28,24},{5,1},{9,5},{13... | collective-permute-start | bytes 393224 | tf_op jit(solution)/shard_map/ppermute | solution.py:30
  172.0 7.8 %collective-permute-start.23 = (f32[8,1,8,512]{3,2,1,0:T(8,128)S(1)}, f32[8,1,8,512]{3,2,1,0:T(8,128)S(1)}, u32[]{:S(2)}, u32[]{:S(2)}) collective-permute-start(f32[8,1,8,512]{3,2,1,0:T(8,128)S(1)} %get-tuple-element.301), channel_id=1, source_target_pairs={{0,4},{4,8},{8,12},{12,16},{16,20},{20,24},{24,28},{1,5},{5,9},{9,... | collective-permute-start | bytes 393224 | tf_op jit(solution)/shard_map/ppermute | solution.py:28
  181.9 5.6 %collective-permute-start.25 = (f32[8,4,1,512]{3,2,1,0:T(1,128)S(1)}, f32[8,4,1,512]{3,2,1,0:T(1,128)S(1)}, u32[]{:S(2)}, u32[]{:S(2)}) collective-permute-start(f32[8,4,1,512]{3,2,1,0:T(1,128)S(1)} %get-tuple-element.277), channel_id=1, source_target_pairs={{0,1},{1,2},{2,3},{4,5},{5,6},{6,7},{8,9},{9,10},{10,11},{12,13},{... | collective-permute-start | bytes 196616 | tf_op jit(solution)/shard_map/ppermute | solution.py:28
  187.8 8.2 %collective-permute-start.26 = (f32[8,1,8,512]{3,2,1,0:T(8,128)S(1)}, f32[8,1,8,512]{3,2,1,0:T(8,128)S(1)}, u32[]{:S(2)}, u32[]{:S(2)}) collective-permute-start(f32[8,1,8,512]{3,2,1,0:T(8,128)S(1)} %get-tuple-element.298), channel_id=1, source_target_pairs={{4,0},{8,4},{12,8},{16,12},{20,16},{24,20},{28,24},{5,1},{9,5},{13... | collective-permute-start | bytes 393224 | tf_op jit(solution)/shard_map/ppermute | solution.py:30
  189.7 7.8 %collective-permute-start.27 = (f32[8,1,8,512]{3,2,1,0:T(8,128)S(1)}, f32[8,1,8,512]{3,2,1,0:T(8,128)S(1)}, u32[]{:S(2)}, u32[]{:S(2)}) collective-permute-start(f32[8,1,8,512]{3,2,1,0:T(8,128)S(1)} %get-tuple-element.297), channel_id=1, source_target_pairs={{0,4},{4,8},{8,12},{12,16},{16,20},{20,24},{24,28},{1,5},{5,9},{9,... | collective-permute-start | bytes 393224 | tf_op jit(solution)/shard_map/ppermute | solution.py:28
  199.5 5.6 %collective-permute-start.29 = (f32[8,4,1,512]{3,2,1,0:T(1,128)S(1)}, f32[8,4,1,512]{3,2,1,0:T(1,128)S(1)}, u32[]{:S(2)}, u32[]{:S(2)}) collective-permute-start(f32[8,4,1,512]{3,2,1,0:T(1,128)S(1)} %get-tuple-element.275), channel_id=1, source_target_pairs={{0,1},{1,2},{2,3},{4,5},{5,6},{6,7},{8,9},{9,10},{10,11},{12,13},{... | collective-permute-start | bytes 196616 | tf_op jit(solution)/shard_map/ppermute | solution.py:28
  276.8 7.8 %collective-permute-start.30 = (f32[8,1,8,512]{3,2,1,0:T(8,128)S(1)}, f32[8,1,8,512]{3,2,1,0:T(8,128)S(1)}, u32[]{:S(2)}, u32[]{:S(2)}) collective-permute-start(f32[8,1,8,512]{3,2,1,0:T(8,128)S(1)} %get-tuple-element.294), channel_id=1, source_target_pairs={{4,0},{8,4},{12,8},{16,12},{20,16},{24,20},{28,24},{5,1},{9,5},{13... | collective-permute-start | bytes 393224 | tf_op jit(solution)/shard_map/ppermute | solution.py:30
  281.4 6.9 %collective-permute-start.31 = (f32[8,1,8,512]{3,2,1,0:T(8,128)S(1)}, f32[8,1,8,512]{3,2,1,0:T(8,128)S(1)}, u32[]{:S(2)}, u32[]{:S(2)}) collective-permute-start(f32[8,1,8,512]{3,2,1,0:T(8,128)S(1)} %get-tuple-element.293), channel_id=1, source_target_pairs={{0,4},{4,8},{8,12},{12,16},{16,20},{20,24},{24,28},{1,5},{5,9},{9,... | collective-permute-start | bytes 393224 | tf_op jit(solution)/shard_map/ppermute | solution.py:28
  (11 other events, 61.6 us)
where the time goes:
time: 298 us; the launch traced here: 297 us
  starting transfers between devices  95.1 us (32%)
  local copies, waits for them, and re-layouts  66.9 us (22%)
  blocking collectives  61.9 us (21%)
  waiting for transfers between devices  46.4 us (16%)
  other arithmetic  19.8 us (7%)
  matrix products  5.65 us (2%)
    all_gather x2, blocking collectives, per_device(): gathered = lax.all_gather(first, 'slab', axis=1, tiled=True)  61.9 us
    gather x2, local copies, waits for them, and re-layouts, per_device(): correction = jnp.take(second, flat_ids, axis=1).reshape(LABELS, CZ, CY, NX)  55.7 us
    ppermute x16, starting transfers between devices, padded(): lax.ppermute(tail, axis, [(i, (i + 1) % count) for i in range(ends)])  52.2 us
    ppermute x16, waiting for transfers between devices, padded(): lax.ppermute(tail, axis, [(i, (i + 1) % count) for i in range(ends)])  39 us
    ppermute x16, starting transfers between devices, padded(): lax.ppermute(head, axis, [((i + 1) % count, i) for i in range(ends)])  38.5 us
    select_n x2, other arithmetic, per_device(): correction = jnp.take(second, flat_ids, axis=1).reshape(LABELS, CZ, CY, NX)  14.9 us
    ppermute x16, waiting for transfers between devices, padded(): lax.ppermute(head, axis, [((i + 1) % count, i) for i in range(ends)])  7.38 us
  transfers between devices with their start and end apart: 34, of which 22 were waited for; matrix products, arithmetic and copies ran while one was open for 2% of the time, Pallas kernels for 0%

commit v1 on v0

--- a/solution.py
+++ b/solution.py
@@ -15,6 +15,36 @@
 smooth_step = 0.8
 coarse_step = 0.7
 weight_unit = 0.125
+
+
+def process_halves_all(message, dim_no):
+    ready = list(message.shape[1:])
+    ready[dim_no] *= message.shape[0]
+    return jnp.moveaxis(message, 0, dim_no).reshape(ready)
+
+
+def wait_bands_up(along_dim, slab_in, mesh_dim):
+    found = []
+    cores_n = jax.lax.axis_size(mesh_dim)
+    for c in [*range(cores_n)]:
+        found.append((c, (c + 1) % cores_n))
+    all_blocks = []
+    for q, src_i in found:
+        all_blocks.append((src_i, q))
+    right_arr, carry_out = ([], [])
+    for m in tuple(range(cores_n - 1)):
+        if m % 2 == 0:
+            then = jax.lax.ppermute(right_arr[-1] if right_arr else slab_in, mesh_dim, found)
+            right_arr.append(then)
+        else:
+            upper = jax.lax.ppermute(carry_out[-1] if carry_out else slab_in, mesh_dim, all_blocks)
+            carry_out.append(upper)
+    v_now = jnp.stack([*right_arr[::-1], slab_in, *carry_out], axis=0)
+    tile_out = jax.lax.axis_index(mesh_dim)
+    e_now = len(right_arr)
+    raw_out = tile_out - e_now
+    v_now = v_now[(jnp.arange(cores_n) - raw_out) % cores_n]
+    return process_halves_all(v_now, along_dim)
 
 
 def padded(cells, sides, width):
@@ -140,7 +170,7 @@
             0, cells // span, collect_block, jnp.zeros((LABELS, CC), jnp.float32)
         )
         first = coarse_step * coarse_rhs / coarse_diag
-        gathered = lax.all_gather(first, "slab", axis=1, tiled=True)
+        gathered = wait_bands_up(1, first, "slab")
         arranged = gathered.reshape(LABELS, group, sections, CC)
         section = lax.dynamic_slice_in_dim(arranged, section_id, 1, 2).reshape(LABELS, group * CC)
         second = (

time: 298 us -> 283 us (0.950)
  blocking collectives: 61.9 us -> 0 us
  starting transfers between devices: 95.1 us -> 127 us
  waiting for transfers between devices: 46.4 us -> 60.7 us
    all_gather x2 -> x0, blocking collectives: 61.9 us -> none  [per_device(): gathered = lax.all_gather(first, 'slab', axis=1, tiled=True)]
    ppermute x0 -> x14, starting transfers between devices: none -> 30.5 us  [the longest x8 23.8 us: wait_bands_up(): jax.lax.ppermute(right_arr[-1] if right_arr else slab_in, mesh_dim, found)]
    ppermute x0 -> x14, waiting for transfers between devices: none -> 12.6 us  [the longest x8 11.3 us: wait_bands_up(): jax.lax.ppermute(right_arr[-1] if right_arr else slab_in, mesh_dim, found)]
  transfers between devices with their start and end apart: 34 -> 48, of which waited for: 22 -> 33; matrix products, arithmetic and copies ran while one was open for 2% -> 2% of each run, Pallas kernels for 0% -> 0%
where the time goes in v1:
time: 283 us; the launch traced here: 281 us
  starting transfers between devices  127 us (45%)
  local copies, waits for them, and re-layouts  67.1 us (24%)
  waiting for transfers between devices  60.7 us (21%)
  other arithmetic  19.9 us (7%)
  matrix products  5.66 us (2%)
    gather x2, local copies, waits for them, and re-layouts, per_device(): correction = jnp.take(second, flat_ids, axis=1).reshape(LABELS, CZ, CY, NX)  55.5 us
    ppermute x16, starting transfers between devices, padded(): lax.ppermute(tail, axis, [(i, (i + 1) % count) for i in range(ends)])  50.9 us
    ppermute x16, starting transfers between devices, padded(): lax.ppermute(head, axis, [((i + 1) % count, i) for i in range(ends)])  41 us
    ppermute x16, waiting for transfers between devices, padded(): lax.ppermute(tail, axis, [(i, (i + 1) % count) for i in range(ends)])  40.8 us
    ppermute x8, starting transfers between devices, wait_bands_up(): jax.lax.ppermute(right_arr[-1] if right_arr else slab_in, mesh_dim, found)  23.8 us
    select_n x2, other arithmetic, per_device(): correction = jnp.take(second, flat_ids, axis=1).reshape(LABELS, CZ, CY, NX)  14.9 us
    ppermute x8, waiting for transfers between devices, wait_bands_up(): jax.lax.ppermute(right_arr[-1] if right_arr else slab_in, mesh_dim, found)  11.3 us
    ppermute x6, starting transfers between devices, wait_bands_up(): jax.lax.ppermute(carry_out[-1] if carry_out else slab_in, mesh_dim, all_b...  6.68 us
  transfers between devices with their start and end apart: 48, of which 33 were waited for; matrix products, arithmetic and copies ran while one was open for 2% of the time, Pallas kernels for 0%

profile of v1, /device:TPU:6, one launch (start us, length us, event | category | flops | bytes accessed | tf_op | source)
XLA Modules:
  0.0 281.3 jit_solution(2108593669914386730)
XLA Ops:
  2.6 4.3 %collective-permute-start.3 = (f32[8,1,8,512]{3,2,1,0:T(8,128)S(1)}, f32[8,1,8,512]{3,2,1,0:T(8,128)S(1)}, u32[]{:S(2)}, u32[]{:S(2)}) collective-permute-start(f32[8,1,8,512]{3,2,1,0:T(8,128)S(1)} %broadcast.209), channel_id=1, source_target_pairs={{0,4},{4,8},{8,12},{12,16},{16,20},{20,24},{24,28},{1,5},{5,9},{9,... | collective-permute-start | bytes 393224 | tf_op jit(solution)/shard_map/ppermute | solution.py:58
  20.8 3.1 %collective-permute-done.5 = f32[8,4,1,512]{3,2,1,0:T(1,128)S(1)} collective-permute-done((f32[8,4,1,512]{3,2,1,0:T(1,128)S(1)}, f32[8,4,1,512]{3,2,1,0:T(1,128)S(1)}, u32[]{:S(2)}, u32[]{:S(2)}) %collective-permute-start.5) | collective-permute-done | bytes 65568 | tf_op jit(solution)/shard_map/ppermute | solution.py:58
  24.2 3.3 %collective-permute-start.6 = (f32[8,1,8,512]{3,2,1,0:T(8,128)S(1)}, f32[8,1,8,512]{3,2,1,0:T(8,128)S(1)}, u32[]{:S(2)}, u32[]{:S(2)}) collective-permute-start(f32[8,1,8,512]{3,2,1,0:T(8,128)S(1)} %get-tuple-element.318), channel_id=1, source_target_pairs={{4,0},{8,4},{12,8},{16,12},{20,16},{24,20},{28,24},{5,1},{9,5},{13... | collective-permute-start | bytes 393224 | tf_op jit(solution)/shard_map/ppermute | solution.py:60
  27.4 3.5 %collective-permute-start.7 = (f32[8,1,8,512]{3,2,1,0:T(8,128)S(1)}, f32[8,1,8,512]{3,2,1,0:T(8,128)S(1)}, u32[]{:S(2)}, u32[]{:S(2)}) collective-permute-start(f32[8,1,8,512]{3,2,1,0:T(8,128)S(1)} %get-tuple-element.317), channel_id=1, source_target_pairs={{0,4},{4,8},{8,12},{12,16},{16,20},{20,24},{24,28},{1,5},{5,9},{9,... | collective-permute-start | bytes 393224 | tf_op jit(solution)/shard_map/ppermute | solution.py:58
  44.1 4.8 %collective-permute-start.11 = (f32[8,1,8,512]{3,2,1,0:T(8,128)S(1)}, f32[8,1,8,512]{3,2,1,0:T(8,128)S(1)}, u32[]{:S(2)}, u32[]{:S(2)}) collective-permute-start(f32[8,1,8,512]{3,2,1,0:T(8,128)S(1)} %get-tuple-element.313), channel_id=1, source_target_pairs={{0,4},{4,8},{8,12},{12,16},{16,20},{20,24},{24,28},{1,5},{5,9},{9,... | collective-permute-start | bytes 393224 | tf_op jit(solution)/shard_map/ppermute | solution.py:58
  62.0 3.4 %collective-permute-start.14 = (f32[8,128]{1,0:T(8,128)S(1)}, f32[8,128]{1,0:T(8,128)S(1)}, u32[]{:S(2)}, u32[]{:S(2)}) collective-permute-start(f32[8,128]{1,0:T(8,128)S(1)} %multiply_divide_fusion.1), channel_id=1, source_target_pairs={{0,4},{4,8},{8,12},{12,16},{16,20},{20,24},{24,28},{28,0},{1,5},{5... | collective-permute-start | bytes 12296 | tf_op jit(solution)/shard_map/ppermute | solution.py:37
  66.7 3.2 %collective-permute-start.15 = (f32[8,128]{1,0:T(8,128)S(1)}, f32[8,128]{1,0:T(8,128)S(1)}, u32[]{:S(2)}, u32[]{:S(2)}) collective-permute-start(f32[8,128]{1,0:T(8,128)S(1)} %collective-permute-done.14), channel_id=1, source_target_pairs={{0,4},{4,8},{8,12},{12,16},{16,20},{20,24},{24,28},{28,0},{1,5},{5... | collective-permute-start | bytes 12296 | tf_op jit(solution)/shard_map/ppermute | solution.py:37
  71.3 3.2 %collective-permute-start.16 = (f32[8,128]{1,0:T(8,128)S(1)}, f32[8,128]{1,0:T(8,128)S(1)}, u32[]{:S(2)}, u32[]{:S(2)}) collective-permute-start(f32[8,128]{1,0:T(8,128)S(1)} %collective-permute-done.15), channel_id=1, source_target_pairs={{0,4},{4,8},{8,12},{12,16},{16,20},{20,24},{24,28},{28,0},{1,5},{5... | collective-permute-start | bytes 12296 | tf_op jit(solution)/shard_map/ppermute | solution.py:37
  79.0 3.4 %collective-permute-start.20 = (f32[8,128]{1,0:T(8,128)S(1)}, f32[8,128]{1,0:T(8,128)S(1)}, u32[]{:S(2)}, u32[]{:S(2)}) collective-permute-start(f32[8,128]{1,0:T(8,128)S(1)} %collective-permute-done.19), channel_id=1, source_target_pairs={{4,0},{8,4},{12,8},{16,12},{20,16},{24,20},{28,24},{0,28},{5,1},{9... | collective-permute-start | bytes 12296 | tf_op jit(solution)/shard_map/ppermute | solution.py:40
  85.1 27.8 %gather_fusion.3 = f32[8192,8]{1,0:T(8,128)} fusion(f32[8,128]{0,1:T(8,128)S(1)} %copy.9, s32[8192]{0:T(1024)S(1)} %fusion.124), kind=kCustom, calls=%fused_computation.clone | custom fusion | bytes 557056 | tf_op jit(solution)/shard_map/jit(_take)/gather | solution.py:191
  112.9 7.5 %broadcast_select_fusion.1 = f32[8192,8]{1,0:T(8,128)} fusion(f32[8192,8]{1,0:T(8,128)} %gather_fusion.3, pred[8192]{0:T(1024)(128)(4,1)S(1)} %compare_and_fusion), kind=kLoop, calls=%fused_computation.18 | loop fusion | flops 65536 | bytes 532480 | tf_op jit(solution)/shard_map/jit(_take)/select_n | solution.py:191
  123.3 6.6 %collective-permute-start.21 = (f32[8,1,8,512]{3,2,1,0:T(8,128)S(1)}, f32[8,1,8,512]{3,2,1,0:T(8,128)S(1)}, u32[]{:S(2)}, u32[]{:S(2)}) collective-permute-start(f32[8,1,8,512]{3,2,1,0:T(8,128)S(1)} %get-tuple-element.310), channel_id=1, source_target_pairs={{4,0},{8,4},{12,8},{16,12},{20,16},{24,20},{28,24},{5,1},{9,5},{13... | collective-permute-start | bytes 393224 | tf_op jit(solution)/shard_map/ppermute | solution.py:60
  132.4 4.4 %collective-permute-done.22 = f32[8,1,8,512]{3,2,1,0:T(8,128)S(1)} collective-permute-done((f32[8,1,8,512]{3,2,1,0:T(8,128)S(1)}, f32[8,1,8,512]{3,2,1,0:T(8,128)S(1)}, u32[]{:S(2)}, u32[]{:S(2)}) %collective-permute-start.22) | collective-permute-done | bytes 131104 | tf_op jit(solution)/shard_map/ppermute | solution.py:58
  146.6 4.8 %collective-permute-start.26 = (f32[8,1,8,512]{3,2,1,0:T(8,128)S(1)}, f32[8,1,8,512]{3,2,1,0:T(8,128)S(1)}, u32[]{:S(2)}, u32[]{:S(2)}) collective-permute-start(f32[8,1,8,512]{3,2,1,0:T(8,128)S(1)} %get-tuple-element.305), channel_id=1, source_target_pairs={{0,4},{4,8},{8,12},{12,16},{16,20},{20,24},{24,28},{1,5},{5,9},{9,... | collective-permute-start | bytes 393224 | tf_op jit(solution)/shard_map/ppermute | solution.py:58
  163.8 5.3 %collective-permute-start.30 = (f32[8,1,8,512]{3,2,1,0:T(8,128)S(1)}, f32[8,1,8,512]{3,2,1,0:T(8,128)S(1)}, u32[]{:S(2)}, u32[]{:S(2)}) collective-permute-start(f32[8,1,8,512]{3,2,1,0:T(8,128)S(1)} %get-tuple-element.301), channel_id=1, source_target_pairs={{0,4},{4,8},{8,12},{12,16},{16,20},{20,24},{24,28},{1,5},{5,9},{9,... | collective-permute-start | bytes 393224 | tf_op jit(solution)/shard_map/ppermute | solution.py:58
  181.5 5.2 %collective-permute-start.34 = (f32[8,1,8,512]{3,2,1,0:T(8,128)S(1)}, f32[8,1,8,512]{3,2,1,0:T(8,128)S(1)}, u32[]{:S(2)}, u32[]{:S(2)}) collective-permute-start(f32[8,1,8,512]{3,2,1,0:T(8,128)S(1)} %get-tuple-element.297), channel_id=1, source_target_pairs={{0,4},{4,8},{8,12},{12,16},{16,20},{20,24},{24,28},{1,5},{5,9},{9,... | collective-permute-start | bytes 393224 | tf_op jit(solution)/shard_map/ppermute | solution.py:58
  199.7 3.3 %collective-permute-start.37 = (f32[8,128]{1,0:T(8,128)S(1)}, f32[8,128]{1,0:T(8,128)S(1)}, u32[]{:S(2)}, u32[]{:S(2)}) collective-permute-start(f32[8,128]{1,0:T(8,128)S(1)} %multiply_divide_fusion), channel_id=1, source_target_pairs={{0,4},{4,8},{8,12},{12,16},{16,20},{20,24},{24,28},{28,0},{1,5},{5... | collective-permute-start | bytes 12296 | tf_op jit(solution)/shard_map/ppermute | solution.py:37
  204.4 3.2 %collective-permute-start.38 = (f32[8,128]{1,0:T(8,128)S(1)}, f32[8,128]{1,0:T(8,128)S(1)}, u32[]{:S(2)}, u32[]{:S(2)}) collective-permute-start(f32[8,128]{1,0:T(8,128)S(1)} %collective-permute-done.37), channel_id=1, source_target_pairs={{0,4},{4,8},{8,12},{12,16},{16,20},{20,24},{24,28},{28,0},{1,5},{5... | collective-permute-start | bytes 12296 | tf_op jit(solution)/shard_map/ppermute | solution.py:37
  208.9 3.2 %collective-permute-start.39 = (f32[8,128]{1,0:T(8,128)S(1)}, f32[8,128]{1,0:T(8,128)S(1)}, u32[]{:S(2)}, u32[]{:S(2)}) collective-permute-start(f32[8,128]{1,0:T(8,128)S(1)} %collective-permute-done.38), channel_id=1, source_target_pairs={{0,4},{4,8},{8,12},{12,16},{16,20},{20,24},{24,28},{28,0},{1,5},{5... | collective-permute-start | bytes 12296 | tf_op jit(solution)/shard_map/ppermute | solution.py:37
  213.5 3.0 %collective-permute-start.40 = (f32[8,128]{1,0:T(8,128)S(1)}, f32[8,128]{1,0:T(8,128)S(1)}, u32[]{:S(2)}, u32[]{:S(2)}) collective-permute-start(f32[8,128]{1,0:T(8,128)S(1)} %collective-permute-done.39), channel_id=1, source_target_pairs={{0,4},{4,8},{8,12},{12,16},{16,20},{20,24},{24,28},{28,0},{1,5},{5... | collective-permute-start | bytes 12296 | tf_op jit(solution)/shard_map/ppermute | solution.py:37
  222.3 27.8 %gather_fusion.4 = f32[8192,8]{1,0:T(8,128)} fusion(f32[8,128]{0,1:T(8,128)S(1)} %copy.11, s32[8192]{0:T(1024)S(1)} %fusion.124), kind=kCustom, calls=%fused_computation.1.clone | custom fusion | bytes 557056 | tf_op jit(solution)/shard_map/jit(_take)/gather | solution.py:191
  250.0 7.5 %broadcast_select_fusion = f32[8192,8]{1,0:T(8,128)} fusion(f32[8192,8]{1,0:T(8,128)} %gather_fusion.4, pred[8192]{0:T(1024)(128)(4,1)S(1)} %compare_and_fusion), kind=kLoop, calls=%fused_computation.17 | loop fusion | flops 65536 | bytes 532480 | tf_op jit(solution)/shard_map/jit(_take)/select_n | solution.py:191
  260.4 5.4 %collective-permute-start.44 = (f32[8,1,8,512]{3,2,1,0:T(8,128)S(1)}, f32[8,1,8,512]{3,2,1,0:T(8,128)S(1)}, u32[]{:S(2)}, u32[]{:S(2)}) collective-permute-start(f32[8,1,8,512]{3,2,1,0:T(8,128)S(1)} %get-tuple-element.294), channel_id=1, source_target_pairs={{4,0},{8,4},{12,8},{16,12},{20,16},{24,20},{28,24},{5,1},{9,5},{13... | collective-permute-start | bytes 393224 | tf_op jit(solution)/shard_map/ppermute | solution.py:60
  268.4 4.4 %collective-permute-done.45 = f32[8,1,8,512]{3,2,1,0:T(8,128)S(1)} collective-permute-done((f32[8,1,8,512]{3,2,1,0:T(8,128)S(1)}, f32[8,1,8,512]{3,2,1,0:T(8,128)S(1)}, u32[]{:S(2)}, u32[]{:S(2)}) %collective-permute-start.45) | collective-permute-done | bytes 131104 | tf_op jit(solution)/shard_map/ppermute | solution.py:58
  (187 shorter events, 133.9 us)
Async XLA Ops:
  0.0 16.2 %collective-permute-start.2 = (f32[8,1,8,512]{3,2,1,0:T(8,128)S(1)}, f32[8,1,8,512]{3,2,1,0:T(8,128)S(1)}, u32[]{:S(2)}, u32[]{:S(2)}) collective-permute-start(f32[8,1,8,512]{3,2,1,0:T(8,128)S(1)} %broadcast.209), channel_id=1, source_target_pairs={{4,0},{8,4},{12,8},{16,12},{20,16},{24,20},{28,24},{5,1},{9,5},{13... | collective-permute-start | bytes 393224 | tf_op jit(solution)/shard_map/ppermute | solution.py:60
  2.6 13.6 %collective-permute-start.3 = (f32[8,1,8,512]{3,2,1,0:T(8,128)S(1)}, f32[8,1,8,512]{3,2,1,0:T(8,128)S(1)}, u32[]{:S(2)}, u32[]{:S(2)}) collective-permute-start(f32[8,1,8,512]{3,2,1,0:T(8,128)S(1)} %broadcast.209), channel_id=1, source_target_pairs={{0,4},{4,8},{8,12},{12,16},{16,20},{20,24},{24,28},{1,5},{5,9},{9,... | collective-permute-start | bytes 393224 | tf_op jit(solution)/shard_map/ppermute | solution.py:58
  7.6 6.3 %collective-permute-start = (s32[1,8,512]{2,1,0:T(8,128)S(1)}, s32[1,8,512]{2,1,0:T(8,128)S(1)}, u32[]{:S(2)}, u32[]{:S(2)}) collective-permute-start(s32[1,8,512]{2,1,0:T(8,128)S(1)} %slice_bitcast_fusion.4), channel_id=1, source_target_pairs={{0,4},{4,8},{8,12},{12,16},{16,20},{20,24},{24,28},{1,5},{5,9},{9,... | collective-permute-start | bytes 49160 | tf_op jit(solution)/shard_map/ppermute | solution.py:70
  18.3 5.6 %collective-permute-start.5 = (f32[8,4,1,512]{3,2,1,0:T(1,128)S(1)}, f32[8,4,1,512]{3,2,1,0:T(1,128)S(1)}, u32[]{:S(2)}, u32[]{:S(2)}) collective-permute-start(f32[8,4,1,512]{3,2,1,0:T(1,128)S(1)} %get-tuple-element.287), channel_id=1, source_target_pairs={{0,1},{1,2},{2,3},{4,5},{5,6},{6,7},{8,9},{9,10},{10,11},{12,13},{... | collective-permute-start | bytes 196616 | tf_op jit(solution)/shard_map/ppermute | solution.py:58
  24.2 7.9 %collective-permute-start.6 = (f32[8,1,8,512]{3,2,1,0:T(8,128)S(1)}, f32[8,1,8,512]{3,2,1,0:T(8,128)S(1)}, u32[]{:S(2)}, u32[]{:S(2)}) collective-permute-start(f32[8,1,8,512]{3,2,1,0:T(8,128)S(1)} %get-tuple-element.318), channel_id=1, source_target_pairs={{4,0},{8,4},{12,8},{16,12},{20,16},{24,20},{28,24},{5,1},{9,5},{13... | collective-permute-start | bytes 393224 | tf_op jit(solution)/shard_map/ppermute | solution.py:60
  27.4 6.9 %collective-permute-start.7 = (f32[8,1,8,512]{3,2,1,0:T(8,128)S(1)}, f32[8,1,8,512]{3,2,1,0:T(8,128)S(1)}, u32[]{:S(2)}, u32[]{:S(2)}) collective-permute-start(f32[8,1,8,512]{3,2,1,0:T(8,128)S(1)} %get-tuple-element.317), channel_id=1, source_target_pairs={{0,4},{4,8},{8,12},{12,16},{16,20},{20,24},{24,28},{1,5},{5,9},{9,... | collective-permute-start | bytes 393224 | tf_op jit(solution)/shard_map/ppermute | solution.py:58
  36.3 5.6 %collective-permute-start.9 = (f32[8,4,1,512]{3,2,1,0:T(1,128)S(1)}, f32[8,4,1,512]{3,2,1,0:T(1,128)S(1)}, u32[]{:S(2)}, u32[]{:S(2)}) collective-permute-start(f32[8,4,1,512]{3,2,1,0:T(1,128)S(1)} %get-tuple-element.285), channel_id=1, source_target_pairs={{0,1},{1,2},{2,3},{4,5},{5,6},{6,7},{8,9},{9,10},{10,11},{12,13},{... | collective-permute-start | bytes 196616 | tf_op jit(solution)/shard_map/ppermute | solution.py:58
  42.2 8.1 %collective-permute-start.10 = (f32[8,1,8,512]{3,2,1,0:T(8,128)S(1)}, f32[8,1,8,512]{3,2,1,0:T(8,128)S(1)}, u32[]{:S(2)}, u32[]{:S(2)}) collective-permute-start(f32[8,1,8,512]{3,2,1,0:T(8,128)S(1)} %get-tuple-element.314), channel_id=1, source_target_pairs={{4,0},{8,4},{12,8},{16,12},{20,16},{24,20},{28,24},{5,1},{9,5},{13... | collective-permute-start | bytes 393224 | tf_op jit(solution)/shard_map/ppermute | solution.py:60
  44.1 7.3 %collective-permute-start.11 = (f32[8,1,8,512]{3,2,1,0:T(8,128)S(1)}, f32[8,1,8,512]{3,2,1,0:T(8,128)S(1)}, u32[]{:S(2)}, u32[]{:S(2)}) collective-permute-start(f32[8,1,8,512]{3,2,1,0:T(8,128)S(1)} %get-tuple-element.313), channel_id=1, source_target_pairs={{0,4},{4,8},{8,12},{12,16},{16,20},{20,24},{24,28},{1,5},{5,9},{9,... | collective-permute-start | bytes 393224 | tf_op jit(solution)/shard_map/ppermute | solution.py:58
  53.5 5.6 %collective-permute-start.13 = (f32[8,4,1,512]{3,2,1,0:T(1,128)S(1)}, f32[8,4,1,512]{3,2,1,0:T(1,128)S(1)}, u32[]{:S(2)}, u32[]{:S(2)}) collective-permute-start(f32[8,4,1,512]{3,2,1,0:T(1,128)S(1)} %get-tuple-element.283), channel_id=1, source_target_pairs={{0,1},{1,2},{2,3},{4,5},{5,6},{6,7},{8,9},{9,10},{10,11},{12,13},{... | collective-permute-start | bytes 196616 | tf_op jit(solution)/shard_map/ppermute | solution.py:58
  71.3 6.3 %collective-permute-start.16 = (f32[8,128]{1,0:T(8,128)S(1)}, f32[8,128]{1,0:T(8,128)S(1)}, u32[]{:S(2)}, u32[]{:S(2)}) collective-permute-start(f32[8,128]{1,0:T(8,128)S(1)} %collective-permute-done.15), channel_id=1, source_target_pairs={{0,4},{4,8},{8,12},{12,16},{16,20},{20,24},{24,28},{28,0},{1,5},{5... | collective-permute-start | bytes 12296 | tf_op jit(solution)/shard_map/ppermute | solution.py:37
  77.6 6.3 %collective-permute-start.17 = (f32[8,128]{1,0:T(8,128)S(1)}, f32[8,128]{1,0:T(8,128)S(1)}, u32[]{:S(2)}, u32[]{:S(2)}) collective-permute-start(f32[8,128]{1,0:T(8,128)S(1)} %collective-permute-done.16), channel_id=1, source_target_pairs={{0,4},{4,8},{8,12},{12,16},{16,20},{20,24},{24,28},{28,0},{1,5},{5... | collective-permute-start | bytes 12296 | tf_op jit(solution)/shard_map/ppermute | solution.py:37
  123.3 9.1 %collective-permute-start.21 = (f32[8,1,8,512]{3,2,1,0:T(8,128)S(1)}, f32[8,1,8,512]{3,2,1,0:T(8,128)S(1)}, u32[]{:S(2)}, u32[]{:S(2)}) collective-permute-start(f32[8,1,8,512]{3,2,1,0:T(8,128)S(1)} %get-tuple-element.310), channel_id=1, source_target_pairs={{4,0},{8,4},{12,8},{16,12},{20,16},{24,20},{28,24},{5,1},{9,5},{13... | collective-permute-start | bytes 393224 | tf_op jit(solution)/shard_map/ppermute | solution.py:60
  129.9 6.9 %collective-permute-start.22 = (f32[8,1,8,512]{3,2,1,0:T(8,128)S(1)}, f32[8,1,8,512]{3,2,1,0:T(8,128)S(1)}, u32[]{:S(2)}, u32[]{:S(2)}) collective-permute-start(f32[8,1,8,512]{3,2,1,0:T(8,128)S(1)} %get-tuple-element.309), channel_id=1, source_target_pairs={{0,4},{4,8},{8,12},{12,16},{16,20},{20,24},{24,28},{1,5},{5,9},{9,... | collective-permute-start | bytes 393224 | tf_op jit(solution)/shard_map/ppermute | solution.py:58
  138.8 5.6 %collective-permute-start.24 = (f32[8,4,1,512]{3,2,1,0:T(1,128)S(1)}, f32[8,4,1,512]{3,2,1,0:T(1,128)S(1)}, u32[]{:S(2)}, u32[]{:S(2)}) collective-permute-start(f32[8,4,1,512]{3,2,1,0:T(1,128)S(1)} %get-tuple-element.281), channel_id=1, source_target_pairs={{0,1},{1,2},{2,3},{4,5},{5,6},{6,7},{8,9},{9,10},{10,11},{12,13},{... | collective-permute-start | bytes 196616 | tf_op jit(solution)/shard_map/ppermute | solution.py:58
  144.7 7.8 %collective-permute-start.25 = (f32[8,1,8,512]{3,2,1,0:T(8,128)S(1)}, f32[8,1,8,512]{3,2,1,0:T(8,128)S(1)}, u32[]{:S(2)}, u32[]{:S(2)}) collective-permute-start(f32[8,1,8,512]{3,2,1,0:T(8,128)S(1)} %get-tuple-element.306), channel_id=1, source_target_pairs={{4,0},{8,4},{12,8},{16,12},{20,16},{24,20},{28,24},{5,1},{9,5},{13... | collective-permute-start | bytes 393224 | tf_op jit(solution)/shard_map/ppermute | solution.py:60
  146.6 7.3 %collective-permute-start.26 = (f32[8,1,8,512]{3,2,1,0:T(8,128)S(1)}, f32[8,1,8,512]{3,2,1,0:T(8,128)S(1)}, u32[]{:S(2)}, u32[]{:S(2)}) collective-permute-start(f32[8,1,8,512]{3,2,1,0:T(8,128)S(1)} %get-tuple-element.305), channel_id=1, source_target_pairs={{0,4},{4,8},{8,12},{12,16},{16,20},{20,24},{24,28},{1,5},{5,9},{9,... | collective-permute-start | bytes 393224 | tf_op jit(solution)/shard_map/ppermute | solution.py:58
  161.8 8.3 %collective-permute-start.29 = (f32[8,1,8,512]{3,2,1,0:T(8,128)S(1)}, f32[8,1,8,512]{3,2,1,0:T(8,128)S(1)}, u32[]{:S(2)}, u32[]{:S(2)}) collective-permute-start(f32[8,1,8,512]{3,2,1,0:T(8,128)S(1)} %get-tuple-element.302), channel_id=1, source_target_pairs={{4,0},{8,4},{12,8},{16,12},{20,16},{24,20},{28,24},{5,1},{9,5},{13... | collective-permute-start | bytes 393224 | tf_op jit(solution)/shard_map/ppermute | solution.py:60
  163.8 7.8 %collective-permute-start.30 = (f32[8,1,8,512]{3,2,1,0:T(8,128)S(1)}, f32[8,1,8,512]{3,2,1,0:T(8,128)S(1)}, u32[]{:S(2)}, u32[]{:S(2)}) collective-permute-start(f32[8,1,8,512]{3,2,1,0:T(8,128)S(1)} %get-tuple-element.301), channel_id=1, source_target_pairs={{0,4},{4,8},{8,12},{12,16},{16,20},{20,24},{24,28},{1,5},{5,9},{9,... | collective-permute-start | bytes 393224 | tf_op jit(solution)/shard_map/ppermute | solution.py:58
  179.5 8.2 %collective-permute-start.33 = (f32[8,1,8,512]{3,2,1,0:T(8,128)S(1)}, f32[8,1,8,512]{3,2,1,0:T(8,128)S(1)}, u32[]{:S(2)}, u32[]{:S(2)}) collective-permute-start(f32[8,1,8,512]{3,2,1,0:T(8,128)S(1)} %get-tuple-element.298), channel_id=1, source_target_pairs={{4,0},{8,4},{12,8},{16,12},{20,16},{24,20},{28,24},{5,1},{9,5},{13... | collective-permute-start | bytes 393224 | tf_op jit(solution)/shard_map/ppermute | solution.py:60
  181.5 7.8 %collective-permute-start.34 = (f32[8,1,8,512]{3,2,1,0:T(8,128)S(1)}, f32[8,1,8,512]{3,2,1,0:T(8,128)S(1)}, u32[]{:S(2)}, u32[]{:S(2)}) collective-permute-start(f32[8,1,8,512]{3,2,1,0:T(8,128)S(1)} %get-tuple-element.297), channel_id=1, source_target_pairs={{0,4},{4,8},{8,12},{12,16},{16,20},{20,24},{24,28},{1,5},{5,9},{9,... | collective-permute-start | bytes 393224 | tf_op jit(solution)/shard_map/ppermute | solution.py:58
  213.5 6.3 %collective-permute-start.40 = (f32[8,128]{1,0:T(8,128)S(1)}, f32[8,128]{1,0:T(8,128)S(1)}, u32[]{:S(2)}, u32[]{:S(2)}) collective-permute-start(f32[8,128]{1,0:T(8,128)S(1)} %collective-permute-done.39), channel_id=1, source_target_pairs={{0,4},{4,8},{8,12},{12,16},{16,20},{20,24},{24,28},{28,0},{1,5},{5... | collective-permute-start | bytes 12296 | tf_op jit(solution)/shard_map/ppermute | solution.py:37
  260.4 8.0 %collective-permute-start.44 = (f32[8,1,8,512]{3,2,1,0:T(8,128)S(1)}, f32[8,1,8,512]{3,2,1,0:T(8,128)S(1)}, u32[]{:S(2)}, u32[]{:S(2)}) collective-permute-start(f32[8,1,8,512]{3,2,1,0:T(8,128)S(1)} %get-tuple-element.294), channel_id=1, source_target_pairs={{4,0},{8,4},{12,8},{16,12},{20,16},{24,20},{28,24},{5,1},{9,5},{13... | collective-permute-start | bytes 393224 | tf_op jit(solution)/shard_map/ppermute | solution.py:60
  265.9 6.9 %collective-permute-start.45 = (f32[8,1,8,512]{3,2,1,0:T(8,128)S(1)}, f32[8,1,8,512]{3,2,1,0:T(8,128)S(1)}, u32[]{:S(2)}, u32[]{:S(2)}) collective-permute-start(f32[8,1,8,512]{3,2,1,0:T(8,128)S(1)} %get-tuple-element.293), channel_id=1, source_target_pairs={{0,4},{4,8},{8,12},{12,16},{16,20},{20,24},{24,28},{1,5},{5,9},{9,... | collective-permute-start | bytes 393224 | tf_op jit(solution)/shard_map/ppermute | solution.py:58
  (26 other events, 195.7 us)
